TPU v7x, 32 devices: a whole 2x2x4 slice. The times are simulated.
32 devices in a mesh: blk: 4 (over x, core), inner: 8 (over z, y).
Axes of the slice: x: 2, y: 2, z: 4, core: 2. Of those that a mesh axis runs over, the one named last changes fastest.
Arguments:
- queries: bfloat16 [4096, 1024], P(('blk', 'inner')), may hold values from -9 to 9
- keys: bfloat16 [4096, 128], P(('blk', 'inner')), may hold values from -4 to 4
- values: bfloat16 [4096, 128], P(('blk', 'inner')), may hold values from -6 to 6
- out_grad: bfloat16 [4096, 1024], P(('blk', 'inner')), may hold values from -6 to 6
- block_list: int32 [32, 5], P(('blk', 'inner')), may hold values from 0 to 31, as said below
Outputs:
- attended: bfloat16 [4096, 1024], P(('blk', 'inner'))
- grad_queries: bfloat16 [4096, 1024], P(('blk', 'inner'))
- grad_keys: float32 [4096, 128], P(('blk', 'inner'))
- grad_values: float32 [4096, 128], P(('blk', 'inner'))
Inputs may be any that keep to these rules, and one draw needn't show every extreme that they name: `block_list`: for query block q, entry n < 2 is max(q - min(n, w - 1), 0) with one w of 2 to 2 a row; each entry n >= 2 is a * 8 for some a with a * 8 <= q.
All inputs are finite; a program needn't handle non-finite values.
Results may differ from a plain program's by a relative error of at most 0.0095.
Values may be sent and summed in bfloat16 or wider, within the bound.
A program may use at most 64 MiB of HBM per device.

v0:
```python
import jax
import jax.numpy as jnp
from jax import lax
from jax.sharding import PartitionSpec as P

HEADS = 8
HEAD_DIM = 128
BLOCK = 128
STRIPES = 3
BAND = 2
NEG = -1e30


def from_behind(block, axis, distance):
    devices = range(lax.axis_size(axis))
    route = [(i - distance, i) for i in devices if i - distance in devices]
    return lax.ppermute(block, axis, route)


def broadcast(value, axis, root):
    mine = lax.axis_index(axis) == root
    return lax.psum(jnp.where(mine, value, jnp.zeros_like(value)), axis)


def shards(queries, keys, values, out_grad, block_list):
    tok_count = keys.shape[0]
    blocks_dev = tok_count // BLOCK
    band_len = BAND
    stripes = STRIPES
    entries = band_len + stripes
    scale = HEAD_DIM ** (-0.5)
    device = lax.axis_index(("blk", "inner"))
    group_blocks = lax.axis_size("inner") * blocks_dev
    groups = lax.axis_size("blk")
    own_blocks = device * blocks_dev + jnp.arange(blocks_dev, dtype=jnp.int32)
    pair = jnp.stack([keys, values])
    earlier = from_behind(pair, ("blk", "inner"), 1)
    window = jnp.concatenate([earlier, pair], axis=1)
    band_pairs = jnp.stack([window])
    column = lax.all_gather(pair[None], "blk", axis=0, tiled=True)
    anchors = broadcast(column, "inner", 0)
    stripe_ids = block_list[:, band_len:]
    anchor_ids = stripe_ids // group_blocks
    picked = anchors[anchor_ids]
    stripe_pairs = jnp.transpose(picked, (0, 2, 1, 3, 4)).reshape(
        blocks_dev, 2, stripes * BLOCK, HEAD_DIM
    )
    key_pairs = jnp.concatenate([band_pairs, stripe_pairs], axis=2)
    band_ids = own_blocks[:, None] - band_len + 1 + jnp.arange(band_len, dtype=jnp.int32)[None, :]
    band_live = (band_ids >= 0) & jnp.any(block_list[:, None, :] == band_ids[:, :, None], axis=2)
    order = jnp.arange(stripes, dtype=jnp.int32)
    before_mask = order[None, :] < order[:, None]
    repeated = jnp.any(
        (stripe_ids[:, :, None] == stripe_ids[:, None, :]) & before_mask[None], axis=2
    )
    in_band = jnp.any(
        (stripe_ids[:, :, None] == band_ids[:, None, :]) & band_live[:, None, :], axis=2
    )
    stripe_live = jnp.logical_not(in_band) & jnp.logical_not(repeated)
    block_live = jnp.concatenate([band_live, stripe_live], axis=1)
    entry_ids = jnp.concatenate([jnp.maximum(band_ids, 0), stripe_ids], axis=1)
    key_tokens = (entry_ids[:, :, None] * BLOCK + jnp.arange(BLOCK, dtype=jnp.int32)).reshape(
        blocks_dev, entries * BLOCK
    )
    live_keys = jnp.repeat(block_live, BLOCK, axis=1)
    query_tokens = own_blocks[:, None] * BLOCK + jnp.arange(BLOCK, dtype=jnp.int32)[None, :]
    allowed = live_keys[:, None, :] & (key_tokens[:, None, :] <= query_tokens[:, :, None])
    heads_per_query = queries.reshape(blocks_dev, BLOCK, HEADS, HEAD_DIM)
    head_gradients = out_grad.reshape(blocks_dev, BLOCK, HEADS, HEAD_DIM)
    key_matrix_rows = key_pairs[:, 0]
    value_matrix_rows = key_pairs[:, 1]
    scores = (
        jnp.einsum(
            "rgao,rmo->ragm", heads_per_query, key_matrix_rows, preferred_element_type=jnp.float32
        )
        * scale
    )
    scores = jnp.where(allowed[:, None], scores, NEG)
    peak = jnp.max(scores, axis=-1, keepdims=True)
    weights = jnp.exp(scores - peak)
    probs = weights / jnp.sum(weights, axis=-1, keepdims=True)
    reduced_probabilities = probs.astype(jnp.bfloat16)
    attended = jnp.einsum(
        "xjaz,xzl->xajl",
        reduced_probabilities,
        value_matrix_rows,
        preferred_element_type=jnp.float32,
    ).astype(jnp.bfloat16)
    grad_probs = jnp.einsum(
        "rgao,rmo->ragm", head_gradients, value_matrix_rows, preferred_element_type=jnp.float32
    )
    delta = jnp.einsum(
        "bihd,bihd->bhi", head_gradients, attended, preferred_element_type=jnp.float32
    )
    score_gradients = (probs * (grad_probs - delta[:, :, :, None]) * scale).astype(jnp.bfloat16)
    grad_queries = jnp.einsum(
        "xjaz,xzl->xajl", score_gradients, key_matrix_rows, preferred_element_type=jnp.float32
    ).astype(jnp.bfloat16)
    grad_key_rows = jnp.einsum(
        "wutc,wtun->wcn", score_gradients, heads_per_query, preferred_element_type=jnp.float32
    )
    grad_value_rows = jnp.einsum(
        "wutc,wtun->wcn", reduced_probabilities, head_gradients, preferred_element_type=jnp.float32
    )
    grad_pairs = jnp.stack([grad_key_rows, grad_value_rows], axis=1)
    window_grad = jnp.zeros((2, 2 * tok_count, HEAD_DIM), jnp.float32)
    begin = tok_count - (band_len - 1) * BLOCK
    window_grad = window_grad.at[:, begin : begin + band_len * BLOCK].add(
        grad_pairs[0, :, : band_len * BLOCK]
    )
    returned = from_behind(
        window_grad[:, :tok_count].astype(jnp.bfloat16), ("blk", "inner"), -1
    ).astype(jnp.float32)
    own_grad = window_grad[:, tok_count:] + returned
    stripe_grads = grad_pairs[:, :, band_len * BLOCK :].reshape(
        blocks_dev, 2, stripes, BLOCK * HEAD_DIM
    )
    stripe_grads = jnp.transpose(stripe_grads, (0, 2, 1, 3)).reshape(
        blocks_dev * stripes, 2, BLOCK * HEAD_DIM
    )
    selector = (
        anchor_ids.reshape(-1)[:, None] == jnp.arange(groups, dtype=jnp.int32)[None, :]
    ).astype(jnp.float32)
    anchor_grad = jnp.einsum("en,exy->nxy", selector, stripe_grads, precision=lax.Precision.HIGHEST)
    anchor_grad = anchor_grad.reshape(groups, 2, BLOCK, HEAD_DIM)
    column_grad = lax.psum_scatter(
        anchor_grad.astype(jnp.bfloat16), "blk", scatter_dimension=0, tiled=True
    ).astype(jnp.float32)
    group_grad = lax.psum(column_grad[0], "inner")
    is_root = lax.axis_index("inner") == 0
    own_grad = own_grad.at[:, :BLOCK].add(jnp.where(is_root, group_grad, 0.0))
    return (
        attended.reshape(tok_count, HEADS * HEAD_DIM),
        grad_queries.reshape(tok_count, HEADS * HEAD_DIM),
        own_grad[0],
        own_grad[1],
    )


def solution(mesh):
    in_specs = (
        P(("blk", "inner"), None),
        P(("blk", "inner"), None),
        P(("blk", "inner"), None),
        P(("blk", "inner"), None),
        P(("blk", "inner"), None),
    )
    out_specs = (
        P(("blk", "inner"), None),
        P(("blk", "inner"), None),
        P(("blk", "inner"), None),
        P(("blk", "inner"), None),
    )
    return jax.shard_map(shards, mesh=mesh, in_specs=in_specs, out_specs=out_specs, check_vma=False)
```

profile of v0, /device:TPU:0, one launch (start us, length us, event | category | flops | bytes accessed | tf_op | source)
XLA Modules:
  0.0 206.3 jit_solution(18070775661744440685)
XLA Ops:
  7.2 0.0 copy-start
  7.2 0.0 all-reduce.3.cloned.1.call-start
  7.2 0.8 pad_maximum_fusion.2
  8.0 4.9 %collective-permute-start = (bf16[2,128,128]{2,1,0:T(8,128)(2,1)S(1)}, bf16[2,128,128]{2,1,0:T(8,128)(2,1)S(1)}, u32[]{:S(2)}, u32[]{:S(2)}) collective-permute-start(bf16[2,128,128]{2,1,0:T(8,128)(2,1)S(1)} %pad_maximum_fusion.2), channel_id=1, source_target_pairs={{0,1},{1,2},{2,3},{3,4},{4,5},{5,6},{6,7},{7,8},{8,9},{9,10},{10,1... | collective-permute-start | bytes 196616 | tf_op jit(solution)/shard_map/ppermute | solution.py:17
  12.9 5.8 %all-gather = bf16[8,128,128]{2,1,0:T(8,128)(2,1)S(1)} all-gather(bf16[2,128,128]{2,1,0:T(8,128)(2,1)S(1)} %pad_maximum_fusion.2), channel_id=2, replica_groups=mesh['blk'=4,'inner'=8] {'blk'}, dimensions={0}, use_global_device_ids=true | all-gather | bytes 327680 | tf_op jit(solution)/shard_map/all_gather | solution.py:40
  18.7 0.7 broadcast_select_fusion
  19.4 0.0 all-reduce.3.cloned.1.call-update
  19.5 0.0 reduce-scatter.2.cloned.1.call-start
  19.5 0.7 fusion.40
  20.3 0.8 compare_reduce_fusion
  21.1 0.1 fusion.41
  21.2 0.1 broadcast_reduce_fusion
  21.3 0.2 fusion.36
  21.5 0.2 and_reduce_fusion
  21.7 0.1 add_bitcast_fusion
  21.8 0.1 broadcast_bitcast_fusion
  21.9 0.2 compare_and_fusion
  22.1 0.0 copy-start.6
  22.1 1.7 copy.72
  23.9 0.0 collective-permute-done
  23.9 0.8 maximum_bitcast_fusion.1
  24.7 65.9 %all-reduce.3.cloned.1.call-done = bf16[4,2,128,128]{3,2,1,0:T(8,128)(2,1)} async-done(((bf16[4,2,128,128]{3,2,1,0:T(8,128)(2,1)}), bf16[4,2,128,128]{3,2,1,0:T(8,128)(2,1)}) %all-reduce.3.cloned.1.call-update) | async-done | bytes 262160 | tf_op jit(solution)/shard_map/psum | solution.py:22
  90.5 1.5 gather_fusion
  92.1 0.0 copy-start.3
  92.1 0.0 copy-done
  92.1 0.5 fusion.5
  92.6 0.5 fusion.4
  93.2 0.0 copy-done.3
  93.2 0.0 copy-start.7
  93.2 1.7 bitcast_convert_fusion
  94.9 0.0 copy-done.6
  94.9 0.0 copy-done.7
  94.9 1.5 fusion.15
  96.5 1.3 copy.63
  97.7 1.8 multiply_reduce_fusion
  99.5 0.9 copy.64
  100.4 0.0 copy-start.5
  100.4 2.1 %fusion.6 = bf16[8,128,640]{1,2,0:T(8,128)(2,1)S(1)} fusion(f32[8,128]{1,0:T(8,128)S(1)} %copy.64, f32[8,128]{1,0:T(8,128)S(1)} %fusion.4, f32[8,128]{1,0:T(8,128)S(1)} %get-tuple-element.66, f32[640,128,8]{1,0,2:T(8,128)S(1)} %get-tuple-element.67, pred[128,640]{0,1:T(8,128)(4,1)} %copy-done.6, bf16[1,2,256,128]{3,2,1,0:T(8,128)(2,1)S(1)} %maximum_bitcast_fusion.1, ...), kind=kOutput, calls=%fused_computation.10 | convolution fusion | flops 173342720 | bytes 4616192 | tf_op jit(solution)/shard_map/rgao,rmo->ragm/dot_general | solution.py:89
  102.5 0.0 copy-start.1
  102.5 1.1 copy-done.1
  103.6 0.5 convolution_bitcast_fusion
  104.1 0.0 copy-done.5
  104.1 0.0 copy-start.2
  104.1 0.0 copy-start.4
  104.2 0.2 reshape.556
  104.3 0.6 fusion.18
  104.9 0.0 copy-start.8
  105.0 0.7 copy.90
  105.7 0.0 reduce-scatter.2.cloned.1.call-update
  105.7 0.0 all-reduce.5.cloned.1.call-start
  105.8 1.3 collective-permute-start.1
  107.1 18.1 %reduce-scatter.2.cloned.1.call-done = bf16[1,2,128,128]{3,2,1,0:T(8,128)(2,1)} async-done(((bf16[4,2,128,128]{3,2,1,0:T(8,128)(2,1)}), bf16[1,2,128,128]{3,2,1,0:T(8,128)(2,1)}) %reduce-scatter.2.cloned.1.call-update) | async-done | bytes 65552 | tf_op jit(solution)/shard_map/reduce_scatter | solution.py:126
  125.2 1.5 bitcast_convert_fusion.1
  126.7 0.0 all-reduce.5.cloned.1.call-update
  126.7 0.0 copy-done.2
  126.7 0.0 copy-done.4
  126.7 0.4 convolution_convert_fusion
  127.1 0.0 copy-done.8
  127.2 0.9 copy.54
  128.0 0.8 copy.55
  128.9 0.0 collective-permute-done.1
  128.9 69.3 %all-reduce.5.cloned.1.call-done = f32[2,128,128]{2,1,0:T(8,128)} async-done(((f32[2,128,128]{2,1,0:T(8,128)}), f32[2,128,128]{2,1,0:T(8,128)}) %all-reduce.5.cloned.1.call-update) | async-done | bytes 131088 | tf_op jit(solution)/shard_map/psum | solution.py:129
  198.2 0.9 fusion.32
  199.1 0.7 slice_bitcast_fusion
  (12 shorter events, 0.1 us)
Async XLA Ops:
  7.2 84.9 %copy-start = (bf16[128,1024]{1,0:T(8,128)(2,1)S(1)}, bf16[128,1024]{1,0:T(8,128)(2,1)}, u32[]{:S(2)}) copy-start(bf16[128,1024]{1,0:T(8,128)(2,1)} %param.13) | copy-start | bytes 786436
  7.2 83.3 %all-reduce.3.cloned.1.call-start = ((), (), s32[]{:S(2)}) async-start(), calls=%async_computation.1 | async-start | bytes 524288 | tf_op jit(solution)/shard_map/psum | solution.py:22
  8.0 15.8 %collective-permute-start = (bf16[2,128,128]{2,1,0:T(8,128)(2,1)S(1)}, bf16[2,128,128]{2,1,0:T(8,128)(2,1)S(1)}, u32[]{:S(2)}, u32[]{:S(2)}) collective-permute-start(bf16[2,128,128]{2,1,0:T(8,128)(2,1)S(1)} %pad_maximum_fusion.2), channel_id=1, source_target_pairs={{0,1},{1,2},{2,3},{3,4},{4,5},{5,6},{6,7},{7,8},{8,9},{9,10},{10,1... | collective-permute-start | bytes 196616 | tf_op jit(solution)/shard_map/ppermute | solution.py:17
  19.5 105.7 %reduce-scatter.2.cloned.1.call-start = ((), (), s32[]{:S(2)}) async-start(), calls=%async_computation.2 | async-start | bytes 327680 | tf_op jit(solution)/shard_map/reduce_scatter | solution.py:126
  22.1 72.8 %copy-start.6 = (pred[128,640]{0,1:T(8,128)(4,1)}, pred[128,640]{0,1:T(8,128)(4,1)S(1)}, u32[]{:S(2)}) copy-start(pred[128,640]{0,1:T(8,128)(4,1)S(1)} %compare_and_fusion) | copy-start | bytes 245764
  92.1 1.1 copy-start.3
  93.2 1.7 copy-start.7
  100.4 3.7 %copy-start.5 = (f32[1,1,640,128]{3,2,1,0:T(8,128)S(1)}, f32[1,1,640,128]{3,2,1,0:T(8,128)}, u32[]{:S(2)}) copy-start(f32[1,1,640,128]{3,2,1,0:T(8,128)} %fusion.15) | copy-start | bytes 983044
  102.5 1.1 copy-start.1
  104.1 22.6 %copy-start.2 = (bf16[8,128,640]{1,2,0:T(8,128)(2,1)S(1)}, bf16[8,128,640]{1,2,0:T(8,128)(2,1)}, u32[]{:S(2)}) copy-start(bf16[8,128,640]{1,2,0:T(8,128)(2,1)} %copy-done.1) | copy-start | bytes 3932164
  104.1 22.6 %copy-start.4 = (bf16[1,2,3,128,128]{4,3,2,1,0:T(8,128)(2,1)S(1)}, bf16[1,2,3,128,128]{4,3,2,1,0:T(8,128)(2,1)}, u32[]{:S(2)}) copy-start(bf16[1,2,3,128,128]{4,3,2,1,0:T(8,128)(2,1)} %copy-done.3) | copy-start | bytes 589828
  104.9 22.2 %copy-start.8 = (bf16[128,8,128]{2,0,1:T(8,128)(2,1)S(1)}, bf16[128,8,128]{2,0,1:T(8,128)(2,1)}, u32[]{:S(2)}) copy-start(bf16[128,8,128]{2,0,1:T(8,128)(2,1)} %get-tuple-element.69) | copy-start | bytes 786436
  105.7 92.5 %all-reduce.5.cloned.1.call-start = ((), (), s32[]{:S(2)}) async-start(), calls=%async_computation.3 | async-start | bytes 262144 | tf_op jit(solution)/shard_map/psum | solution.py:129
  105.8 23.0 %collective-permute-start.1 = (bf16[2,128,128]{2,1,0:T(8,128)(2,1)S(1)}, bf16[2,128,128]{2,1,0:T(8,128)(2,1)S(1)}, u32[]{:S(2)}, u32[]{:S(2)}) collective-permute-start(bf16[2,128,128]{2,1,0:T(8,128)(2,1)S(1)} %slice.106), channel_id=1, source_target_pairs={{1,0},{2,1},{3,2},{4,3},{5,4},{6,5},{7,6},{8,7},{9,8},{10,9},{11,1... | collective-permute-start | bytes 196616 | tf_op jit(solution)/shard_map/ppermute | solution.py:17
Sparse Core Ops, SparseCore 0:
  19.6 70.9 all-reduce.2
  105.8 19.2 reduce-scatter.1
  128.5 69.5 all-reduce.4
where the time goes:
time: 207 us; the launch traced here: 206 us
  waiting for transfers between devices  153 us (74%)
  between operations  14 us (7%)
  local copies, waits for them, and re-layouts  10 us (5%)
  other arithmetic  9.53 us (5%)
  matrix products  7.35 us (4%)
  starting transfers between devices  6.27 us (3%)
  blocking collectives  5.79 us (3%)
    psum x1, waiting for transfers between devices, shards(): group_grad = lax.psum(column_grad[0], 'inner')  69.3 us
    psum x1, waiting for transfers between devices, broadcast(): return lax.psum(jnp.where(mine, value, jnp.zeros_like(value)), axis)  65.9 us
    reduce_scatter x1, waiting for transfers between devices, shards(): lax.psum_scatter(anchor_grad.astype(jnp.bfloat16), 'blk', scatter_dimensi...  18.1 us
    ppermute x2, starting transfers between devices, from_behind(): return lax.ppermute(block, axis, route)  6.15 us
    unnamed x22, local copies, waits for them, and re-layouts  5.8 us
    all_gather x1, blocking collectives, shards(): column = lax.all_gather(pair[None], 'blk', axis=0, tiled=True)  5.79 us
  transfers between devices with their start and end apart: 5, of which 3 were waited for; matrix products, arithmetic and copies ran while one was open for 5% of the time, Pallas kernels for 0%

commit v1 on v0

--- a/solution.py
+++ b/solution.py
@@ -2,6 +2,7 @@
 import jax.numpy as jnp
 from jax import lax
 from jax.sharding import PartitionSpec as P
+from jax.lax import all_gather
 
 HEADS = 8
 HEAD_DIM = 128
@@ -9,6 +10,10 @@
 STRIPES = 3
 BAND = 2
 NEG = -1e30
+
+
+def rest_the_knots(z, a_name):
+    return jnp.sum(all_gather(z, a_name), 0)
 
 
 def from_behind(block, axis, distance):
@@ -19,7 +24,7 @@
 
 def broadcast(value, axis, root):
     mine = lax.axis_index(axis) == root
-    return lax.psum(jnp.where(mine, value, jnp.zeros_like(value)), axis)
+    return rest_the_knots(jnp.where(mine, value, jnp.zeros_like(value)), axis)
 
 
 def shards(queries, keys, values, out_grad, block_list):

time: 207 us -> 184 us (0.89)
  waiting for transfers between devices: 153 us -> 129 us
    psum x1 -> x0, waiting for transfers between devices: 65.9 us -> none  [broadcast(): return lax.psum(jnp.where(mine, value, jnp.zeros_like(value)), axis)]
    all_gather x0 -> x1, waiting for transfers between devices: none -> 42.2 us  [rest_the_knots(): return jnp.sum(all_gather(z, a_name), 0)]
where the time goes in v1:
time: 184 us; the launch traced here: 183 us
  waiting for transfers between devices  129 us (70%)
  between operations  14 us (8%)
  other arithmetic  11.5 us (6%)
  local copies, waits for them, and re-layouts  9.01 us (5%)
  matrix products  7.36 us (4%)
  blocking collectives  7.18 us (4%)
  starting transfers between devices  4.88 us (3%)
    psum x1, waiting for transfers between devices, shards(): group_grad = lax.psum(column_grad[0], 'inner')  69.7 us
    all_gather x1, waiting for transfers between devices, rest_the_knots(): return jnp.sum(all_gather(z, a_name), 0)  42.2 us
    reduce_scatter x1, waiting for transfers between devices, shards(): lax.psum_scatter(anchor_grad.astype(jnp.bfloat16), 'blk', scatter_dimensi...  17.3 us
    all_gather x1, blocking collectives, shards(): column = lax.all_gather(pair[None], 'blk', axis=0, tiled=True)  7.18 us
    unnamed x22, local copies, waits for them, and re-layouts  5.77 us
    ppermute x2, starting transfers between devices, from_behind(): return lax.ppermute(block, axis, route)  4.76 us
  transfers between devices with their start and end apart: 5, of which 3 were waited for; matrix products, arithmetic and copies ran while one was open for 5% of the time, Pallas kernels for 0%

profile of v1, /device:TPU:0, one launch (start us, length us, event | category | flops | bytes accessed | tf_op | source)
XLA Modules:
  0.0 183.2 jit_solution(11919831789983466792)
XLA Ops:
  7.2 0.0 copy-start
  7.2 0.0 all-gather.4.cloned.1.call-start
  7.2 0.8 pad_maximum_fusion.2
  8.0 7.2 %all-gather = bf16[8,128,128]{2,1,0:T(8,128)(2,1)S(1)} all-gather(bf16[2,128,128]{2,1,0:T(8,128)(2,1)S(1)} %pad_maximum_fusion.2), channel_id=2, replica_groups=mesh['blk'=4,'inner'=8] {'blk'}, dimensions={0}, use_global_device_ids=true | all-gather | bytes 327680 | tf_op jit(solution)/shard_map/all_gather | solution.py:45
  15.2 0.7 broadcast_select_fusion
  15.9 0.0 all-gather.4.cloned.1.call-update
  16.0 0.0 reduce-scatter.2.cloned.1.call-start
  16.0 3.5 %collective-permute-start = (bf16[2,128,128]{2,1,0:T(8,128)(2,1)S(1)}, bf16[2,128,128]{2,1,0:T(8,128)(2,1)S(1)}, u32[]{:S(2)}, u32[]{:S(2)}) collective-permute-start(bf16[2,128,128]{2,1,0:T(8,128)(2,1)S(1)} %pad_maximum_fusion.2), channel_id=1, source_target_pairs={{0,1},{1,2},{2,3},{3,4},{4,5},{5,6},{6,7},{7,8},{8,9},{9,10},{10,1... | collective-permute-start | bytes 196616 | tf_op jit(solution)/shard_map/ppermute | solution.py:22
  19.5 1.7 copy.72
  21.2 0.7 fusion.40
  22.0 0.1 fusion.41
  22.1 0.2 fusion.36
  22.2 0.8 compare_reduce_fusion
  23.1 0.2 and_reduce_fusion
  23.3 0.1 add_bitcast_fusion
  23.4 0.1 broadcast_reduce_fusion
  23.5 0.1 broadcast_bitcast_fusion
  23.5 0.2 compare_and_fusion
  23.8 0.0 copy-start.6
  23.8 0.0 collective-permute-done
  23.8 0.8 maximum_bitcast_fusion.1
  24.6 42.2 %all-gather.4.cloned.1.call-done = bf16[32,2,128,128]{3,2,1,0:T(8,128)(2,1)} async-done(((bf16[4,2,128,128]{3,2,1,0:T(8,128)(2,1)}), bf16[32,2,128,128]{3,2,1,0:T(8,128)(2,1)}) %all-gather.4.cloned.1.call-update) | async-done | bytes 2097168 | tf_op jit(solution)/shard_map/all_gather | solution.py:16
  66.8 2.0 %reduce_sum.21 = bf16[4,2,128,128]{3,2,1,0:T(8,128)(2,1)S(1)} reduce(bf16[8,4,2,128,128]{4,3,2,1,0:T(8,128)(2,1)} %bitcast.175, bf16[]{:T(256)} %constant.105.clone.1), dimensions={0}, to_apply=%region_0.1 | reduce | flops 917504 | bytes 2359298 | tf_op jit(solution)/shard_map/reduce_sum | solution.py:16
  68.8 0.6 gather_fusion
  69.4 0.0 copy-start.3
  69.4 0.0 copy-done
  69.4 0.5 fusion.5
  70.0 0.5 fusion.4
  70.5 0.0 copy-done.3
  70.5 0.0 copy-start.7
  70.6 1.7 bitcast_convert_fusion
  72.3 0.0 copy-done.6
  72.3 0.0 copy-done.7
  72.3 1.5 fusion.15
  73.8 1.3 copy.63
  75.1 1.8 multiply_reduce_fusion
  76.9 0.9 copy.64
  77.8 2.1 %fusion.6 = bf16[8,128,640]{1,2,0:T(8,128)(2,1)S(1)} fusion(f32[8,128]{1,0:T(8,128)S(1)} %copy.64, f32[8,128]{1,0:T(8,128)S(1)} %fusion.4, f32[8,128]{1,0:T(8,128)S(1)} %get-tuple-element.66, f32[640,128,8]{1,0,2:T(8,128)S(1)} %get-tuple-element.67, pred[128,640]{0,1:T(8,128)(4,1)} %copy-done.6, bf16[1,2,256,128]{3,2,1,0:T(8,128)(2,1)S(1)} %maximum_bitcast_fusion.1, ...), kind=kOutput, calls=%fused_computation.10 | convolution fusion | flops 173342720 | bytes 4616192 | tf_op jit(solution)/shard_map/rgao,rmo->ragm/dot_general | solution.py:94
  79.9 0.0 copy-start.1
  79.9 1.1 copy-done.1
  80.9 0.5 convolution_bitcast_fusion
  81.4 0.0 copy-done.5
  81.4 0.0 copy-start.2
  81.5 0.0 copy-start.4
  81.5 0.2 reshape.556
  81.7 0.6 fusion.18
  82.3 0.0 copy-start.8
  82.3 0.7 copy.90
  83.1 0.0 reduce-scatter.2.cloned.1.call-update
  83.1 0.0 all-reduce.2.cloned.1.call-start
  83.2 1.3 collective-permute-start.1
  84.5 17.3 %reduce-scatter.2.cloned.1.call-done = bf16[1,2,128,128]{3,2,1,0:T(8,128)(2,1)} async-done(((bf16[4,2,128,128]{3,2,1,0:T(8,128)(2,1)}), bf16[1,2,128,128]{3,2,1,0:T(8,128)(2,1)}) %reduce-scatter.2.cloned.1.call-update) | async-done | bytes 65552 | tf_op jit(solution)/shard_map/reduce_scatter | solution.py:131
  101.7 1.5 bitcast_convert_fusion.1
  103.2 0.0 all-reduce.2.cloned.1.call-update
  103.2 0.0 copy-done.2
  103.3 0.0 copy-done.4
  103.3 0.4 convolution_convert_fusion
  103.7 0.0 copy-done.8
  103.7 0.9 copy.54
  104.5 0.8 copy.55
  105.4 0.0 collective-permute-done.1
  105.4 69.7 %all-reduce.2.cloned.1.call-done = f32[2,128,128]{2,1,0:T(8,128)} async-done(((f32[2,128,128]{2,1,0:T(8,128)}), f32[2,128,128]{2,1,0:T(8,128)}) %all-reduce.2.cloned.1.call-update) | async-done | bytes 131088 | tf_op jit(solution)/shard_map/psum | solution.py:134
  175.1 0.9 fusion.32
  176.0 0.7 slice_bitcast_fusion
  (13 shorter events, 0.1 us)
Async XLA Ops:
  7.2 62.3 %copy-start = (bf16[128,1024]{1,0:T(8,128)(2,1)S(1)}, bf16[128,1024]{1,0:T(8,128)(2,1)}, u32[]{:S(2)}) copy-start(bf16[128,1024]{1,0:T(8,128)(2,1)} %param.13) | copy-start | bytes 786436
  7.2 59.7 %all-gather.4.cloned.1.call-start = ((), (), s32[]{:S(2)}) async-start(), calls=%async_computation.3 | async-start | bytes 2359296 | tf_op jit(solution)/shard_map/all_gather | solution.py:16
  16.0 85.8 %reduce-scatter.2.cloned.1.call-start = ((), (), s32[]{:S(2)}) async-start(), calls=%async_computation.1 | async-start | bytes 327680 | tf_op jit(solution)/shard_map/reduce_scatter | solution.py:131
  16.0 7.8 %collective-permute-start = (bf16[2,128,128]{2,1,0:T(8,128)(2,1)S(1)}, bf16[2,128,128]{2,1,0:T(8,128)(2,1)S(1)}, u32[]{:S(2)}, u32[]{:S(2)}) collective-permute-start(bf16[2,128,128]{2,1,0:T(8,128)(2,1)S(1)} %pad_maximum_fusion.2), channel_id=1, source_target_pairs={{0,1},{1,2},{2,3},{3,4},{4,5},{5,6},{6,7},{7,8},{8,9},{9,10},{10,1... | collective-permute-start | bytes 196616 | tf_op jit(solution)/shard_map/ppermute | solution.py:22
  23.8 48.5 %copy-start.6 = (pred[128,640]{0,1:T(8,128)(4,1)}, pred[128,640]{0,1:T(8,128)(4,1)S(1)}, u32[]{:S(2)}) copy-start(pred[128,640]{0,1:T(8,128)(4,1)S(1)} %compare_and_fusion) | copy-start | bytes 245764
  69.4 1.1 copy-start.3
  70.5 1.7 copy-start.7
  77.8 3.7 %copy-start.5 = (f32[1,1,640,128]{3,2,1,0:T(8,128)S(1)}, f32[1,1,640,128]{3,2,1,0:T(8,128)}, u32[]{:S(2)}) copy-start(f32[1,1,640,128]{3,2,1,0:T(8,128)} %fusion.15) | copy-start | bytes 983044
  79.9 1.1 copy-start.1
  81.4 21.8 %copy-start.2 = (bf16[8,128,640]{1,2,0:T(8,128)(2,1)S(1)}, bf16[8,128,640]{1,2,0:T(8,128)(2,1)}, u32[]{:S(2)}) copy-start(bf16[8,128,640]{1,2,0:T(8,128)(2,1)} %copy-done.1) | copy-start | bytes 3932164
  81.5 21.8 %copy-start.4 = (bf16[1,2,3,128,128]{4,3,2,1,0:T(8,128)(2,1)S(1)}, bf16[1,2,3,128,128]{4,3,2,1,0:T(8,128)(2,1)}, u32[]{:S(2)}) copy-start(bf16[1,2,3,128,128]{4,3,2,1,0:T(8,128)(2,1)} %copy-done.3) | copy-start | bytes 589828
  82.3 21.4 %copy-start.8 = (bf16[128,8,128]{2,0,1:T(8,128)(2,1)S(1)}, bf16[128,8,128]{2,0,1:T(8,128)(2,1)}, u32[]{:S(2)}) copy-start(bf16[128,8,128]{2,0,1:T(8,128)(2,1)} %get-tuple-element.69) | copy-start | bytes 786436
  83.1 92.0 %all-reduce.2.cloned.1.call-start = ((), (), s32[]{:S(2)}) async-start(), calls=%async_computation.2 | async-start | bytes 262144 | tf_op jit(solution)/shard_map/psum | solution.py:134
  83.2 22.2 %collective-permute-start.1 = (bf16[2,128,128]{2,1,0:T(8,128)(2,1)S(1)}, bf16[2,128,128]{2,1,0:T(8,128)(2,1)S(1)}, u32[]{:S(2)}, u32[]{:S(2)}) collective-permute-start(bf16[2,128,128]{2,1,0:T(8,128)(2,1)S(1)} %slice.106), channel_id=1, source_target_pairs={{1,0},{2,1},{3,2},{4,3},{5,4},{6,5},{7,6},{8,7},{9,8},{10,9},{11,1... | collective-permute-start | bytes 196616 | tf_op jit(solution)/shard_map/ppermute | solution.py:22
Sparse Core Ops, SparseCore 0:
  16.1 50.6 all-gather.3
  83.2 18.4 reduce-scatter.1
  105.4 69.6 all-reduce.1
